TPU v7x, 32 devices: a whole 2x2x4 slice. The times are simulated.
32 devices in a mesh: gx: 4 (over x, core), gy: 8 (over z, y).
Axes of the slice: x: 2, y: 2, z: 4, core: 2. Of those that a mesh axis runs over, the one named last changes fastest.
Arguments:
- tokens: bfloat16 [2740, 1024], P('gx', 'gy'), may hold values from -64 to 64
- cotangent: bfloat16 [2740, 1024], P('gx', 'gy'), may hold values from -6 to 6
- norm1_gain: float32 [1024], P('gy'), may hold values from 0.1 to 1.9
- norm1_shift: float32 [1024], P('gy'), may hold values from -1.5 to 1.5
- qkv_weight: bfloat16 [1024, 3072], P('gx', 'gy'), may hold values from -4 to 4
- qv_bias: float32 [2048], P('gy'), may hold values from -2.5 to 2.5
- proj_weight: bfloat16 [1024, 1024], P('gx', 'gy'), may hold values from -1.5 to 1.5
- proj_bias: float32 [1024], P('gy'), may hold values from -1.5 to 1.5
- scale_attn: float32 [1024], P('gy'), may hold values from 0.3 to 1.5
- norm2_gain: float32 [1024], P('gy'), may hold values from 0.1 to 1.9
- norm2_shift: float32 [1024], P('gy'), may hold values from -1.5 to 1.5
- fc1_weight: bfloat16 [1024, 4096], P('gx', 'gy'), may hold values from -0.1875 to 0.1875
- fc1_bias: float32 [4096], P('gy'), may hold values from -2.5 to 2.5
- fc2_weight: bfloat16 [4096, 1024], P('gx', 'gy'), may hold values from -0.09375 to 0.09375
- fc2_bias: float32 [1024], P('gy'), may hold values from -1.5 to 1.5
- scale_mlp: float32 [1024], P('gy'), may hold values from 0.3 to 1.5
Outputs:
- output: float32 [2740, 1024], P('gx', 'gy')
- grad_tokens: float32 [2740, 1024], P('gx', 'gy')
- grad_norm1_gain: float32 [1024], P('gy')
- grad_norm1_shift: float32 [1024], P('gy')
- grad_qkv_weight: float32 [1024, 3072], P('gx', 'gy')
- grad_qv_bias: float32 [2048], P('gy')
- grad_proj_weight: float32 [1024, 1024], P('gx', 'gy')
- grad_proj_bias: float32 [1024], P('gy')
- grad_scale_attn: float32 [1024], P('gy')
- grad_norm2_gain: float32 [1024], P('gy')
- grad_norm2_shift: float32 [1024], P('gy')
- grad_fc1_weight: float32 [1024, 4096], P('gx', 'gy')
- grad_fc1_bias: float32 [4096], P('gy')
- grad_fc2_weight: float32 [4096, 1024], P('gx', 'gy')
- grad_fc2_bias: float32 [1024], P('gy')
- grad_scale_mlp: float32 [1024], P('gy')
All inputs are finite; a program needn't handle non-finite values.
Results may differ from a plain program's by a relative error of at most 0.012.
Values may be sent and summed in bfloat16 or wider, within the bound.
A program may use at most 128 MiB of HBM per device.

v0:
```python
import jax
import jax.numpy as jnp
from jax import lax
from jax.sharding import PartitionSpec as P

D = 1024
HD = 64
IMGS = 1
EPS = 1e-06
ROOT_HALF = 0.7071067811865476
INV_ROOT_TAU = 0.3989422804014327


def from_partner(block, axis, bit):
    count = lax.axis_size(axis)
    route = []
    for low in range(count):
        high = low | 1 << bit
        if high != low and high < count:
            route += [(low, high), (high, low)]
    return lax.ppermute(block, axis, route)


def normal_cdf(values):
    return 0.5 * (1.0 + jax.scipy.special.erf(values * ROOT_HALF))


def gelu_exact(values):
    return values * normal_cdf(values)


def gelu_slope(values):
    return normal_cdf(values) + values * jnp.exp(-0.5 * values * values) * INV_ROOT_TAU


def norm_forward(rows, gain, shift):
    totals, squares = lax.psum((jnp.sum(rows, axis=1), jnp.sum(rows * rows, axis=1)), "gy")
    row_mean = totals / D
    inv_std = lax.rsqrt(squares / D - row_mean * row_mean + EPS)[:, None]
    normed = (rows - row_mean[:, None]) * inv_std
    return (normed, inv_std, (normed * gain + shift).astype(jnp.bfloat16))


def norm_backward(grad_normed, normed, inv_std, gain):
    scaled = grad_normed * gain
    first, second = lax.psum((jnp.sum(scaled, axis=1), jnp.sum(scaled * normed, axis=1)), "gy")
    return inv_std * (scaled - first[:, None] / D - normed * (second[:, None] / D))


def project(inputs, weight):
    result = jnp.dot(
        lax.all_gather(inputs, "gy", axis=1, tiled=True), weight, preferred_element_type=jnp.float32
    )
    return (result, inputs)


def weight_grad(saved, grad_out):
    return jnp.einsum(
        "tk,tn->kn",
        lax.all_gather(saved, "gy", axis=1, tiled=True),
        grad_out,
        preferred_element_type=jnp.float32,
    )


def back_project(grad_out, weight):
    term = jnp.einsum("tn,kn->tk", grad_out, weight, preferred_element_type=jnp.float32)
    return lax.psum_scatter(term, "gy", scatter_dimension=1, tiled=True)


def on_device(
    tokens,
    cotangent,
    norm1_gain,
    norm1_shift,
    qkv_weight,
    qv_bias,
    proj_weight,
    proj_bias,
    scale_attn,
    norm2_gain,
    norm2_shift,
    fc1_weight,
    fc1_bias,
    fc2_weight,
    fc2_bias,
    scale_mlp,
):
    count = tokens.shape[0]
    half_len = count // IMGS
    heads_here = qkv_weight.shape[1] // (3 * HD)
    factor = HD ** (-0.5)
    full_qkv, full_proj, full_fc1, full_fc2 = (
        lax.all_gather(qkv_weight, "gx", axis=0, tiled=True),
        lax.all_gather(proj_weight, "gx", axis=0, tiled=True),
        lax.all_gather(fc1_weight, "gx", axis=0, tiled=True),
        lax.all_gather(fc2_weight, "gx", axis=0, tiled=True),
    )
    inputs = tokens.astype(jnp.float32)
    normed_one, inv_one, norm_one = norm_forward(inputs, norm1_gain, norm1_shift)
    mixed, saved_one = project(norm_one, full_qkv)
    mixed = mixed.reshape(count, heads_here, 3, HD)
    biases = qv_bias.reshape(heads_here, 2, HD)
    queries = (mixed[:, :, 0] + biases[:, 0]).astype(jnp.bfloat16)
    keys = mixed[:, :, 1].astype(jnp.bfloat16)
    values = (mixed[:, :, 2] + biases[:, 1]).astype(jnp.bfloat16)
    lower = lax.axis_index("gx") % 2 == 0
    pair_kv = jnp.concatenate([keys, values], axis=2).reshape(count, heads_here * 2 * HD)
    other_kv = from_partner(pair_kv, "gx", 0)
    first_kv = jnp.where(lower, pair_kv, other_kv)
    second_kv = jnp.where(lower, other_kv, pair_kv)
    image_shape = (IMGS, half_len, heads_here, 2 * HD)
    both_kv = jnp.concatenate(
        [first_kv.reshape(image_shape), second_kv.reshape(image_shape)], axis=1
    )
    key_all = both_kv[..., :HD]
    value_all = both_kv[..., HD:]
    query_img = queries.reshape(IMGS, half_len, heads_here, HD)
    scores = (
        jnp.einsum("iqhe,ikhe->ihqk", query_img, key_all, preferred_element_type=jnp.float32)
        * factor
    )
    row_max = jnp.max(scores, axis=3, keepdims=True)
    exponent = jnp.exp(scores - row_max)
    totals = jnp.sum(exponent, axis=3, keepdims=True)
    log_total = row_max + jnp.log(totals)
    probs = (exponent / totals).astype(jnp.bfloat16)
    attended_img = jnp.einsum(
        "ihqk,ikhe->iqhe", probs, value_all, preferred_element_type=jnp.float32
    ).astype(jnp.bfloat16)
    attended = attended_img.reshape(count, heads_here * HD)
    attn_out, saved_two = project(attended, full_proj)
    attn_out = attn_out + proj_bias
    middle = inputs + scale_attn * attn_out
    normed_two, inv_two, norm_two = norm_forward(middle, norm2_gain, norm2_shift)
    pre_act, saved_three = project(norm_two, full_fc1)
    pre_act = pre_act + fc1_bias
    hidden = gelu_exact(pre_act).astype(jnp.bfloat16)
    mlp_out, saved_four = project(hidden, full_fc2)
    mlp_out = mlp_out + fc2_bias
    output = middle + scale_mlp * mlp_out
    upstream = cotangent.astype(jnp.float32)
    grad_scale_mlp = jnp.sum(upstream * mlp_out, axis=0)
    grad_mlp = upstream * scale_mlp
    grad_fc2_bias = jnp.sum(grad_mlp, axis=0)
    grad_mlp_b = grad_mlp.astype(jnp.bfloat16)
    grad_fc2 = weight_grad(saved_four, grad_mlp_b)
    grad_hidden = back_project(grad_mlp_b, full_fc2)
    grad_pre = grad_hidden * gelu_slope(pre_act)
    grad_fc1_bias = jnp.sum(grad_pre, axis=0)
    grad_pre_b = grad_pre.astype(jnp.bfloat16)
    grad_fc1 = weight_grad(saved_three, grad_pre_b)
    grad_norm_two = back_project(grad_pre_b, full_fc1)
    grad_gain_two = jnp.sum(grad_norm_two * normed_two, axis=0)
    grad_shift_two = jnp.sum(grad_norm_two, axis=0)
    grad_middle = upstream + norm_backward(grad_norm_two, normed_two, inv_two, norm2_gain)
    grad_scale_attn = jnp.sum(grad_middle * attn_out, axis=0)
    grad_attn = grad_middle * scale_attn
    grad_proj_bias = jnp.sum(grad_attn, axis=0)
    grad_attn_b = grad_attn.astype(jnp.bfloat16)
    grad_proj = weight_grad(saved_two, grad_attn_b)
    grad_attended = back_project(grad_attn_b, full_proj).astype(jnp.bfloat16)
    grad_att_img = grad_attended.reshape(IMGS, half_len, heads_here, HD)
    recomputed = jnp.exp(scores - log_total)
    probs_b = recomputed.astype(jnp.bfloat16)
    grad_value_all = jnp.einsum(
        "ihqk,iqhe->ikhe", probs_b, grad_att_img, preferred_element_type=jnp.float32
    )
    grad_probs = jnp.einsum(
        "iqhe,ikhe->ihqk", grad_att_img, value_all, preferred_element_type=jnp.float32
    )
    delta = jnp.sum(grad_att_img.astype(jnp.float32) * attended_img.astype(jnp.float32), axis=3)
    grad_scores = recomputed * (grad_probs - jnp.transpose(delta, (0, 2, 1))[..., None])
    grad_scores_b = grad_scores.astype(jnp.bfloat16)
    grad_query = (
        jnp.einsum("ihqk,ikhe->iqhe", grad_scores_b, key_all, preferred_element_type=jnp.float32)
        * factor
    )
    grad_key_all = (
        jnp.einsum("ihqk,iqhe->ikhe", grad_scores_b, query_img, preferred_element_type=jnp.float32)
        * factor
    )
    grad_kv_all = jnp.concatenate([grad_key_all, grad_value_all], axis=3)
    first_part = grad_kv_all[:, :half_len].reshape(count, heads_here * 2 * HD)
    second_part = grad_kv_all[:, half_len:].reshape(count, heads_here * 2 * HD)
    own_part = jnp.where(lower, first_part, second_part)
    sent_part = jnp.where(lower, second_part, first_part)
    grad_kv = own_part + from_partner(sent_part.astype(jnp.bfloat16), "gx", 0).astype(
        sent_part.dtype
    )
    grad_kv = grad_kv.reshape(count, heads_here, 2, HD)
    grad_query = grad_query.reshape(count, heads_here, HD)
    grad_qv_bias = jnp.stack(
        [jnp.sum(grad_query, axis=0), jnp.sum(grad_kv[:, :, 1], axis=0)], axis=1
    ).reshape(heads_here * 2 * HD)
    grad_mixed = (
        jnp.stack([grad_query, grad_kv[:, :, 0], grad_kv[:, :, 1]], axis=2)
        .astype(jnp.bfloat16)
        .reshape(count, heads_here * 3 * HD)
    )
    grad_qkv = weight_grad(saved_one, grad_mixed)
    grad_norm_one = back_project(grad_mixed, full_qkv)
    grad_gain_one = jnp.sum(grad_norm_one * normed_one, axis=0)
    grad_shift_one = jnp.sum(grad_norm_one, axis=0)
    grad_input = grad_middle + norm_backward(grad_norm_one, normed_one, inv_one, norm1_gain)
    grad_qkv, grad_proj, grad_fc1, grad_fc2 = (
        lax.psum_scatter(
            grad_qkv.astype(jnp.bfloat16), "gx", scatter_dimension=0, tiled=True
        ).astype(jnp.float32),
        lax.psum_scatter(
            grad_proj.astype(jnp.bfloat16), "gx", scatter_dimension=0, tiled=True
        ).astype(jnp.float32),
        lax.psum_scatter(
            grad_fc1.astype(jnp.bfloat16), "gx", scatter_dimension=0, tiled=True
        ).astype(jnp.float32),
        lax.psum_scatter(
            grad_fc2.astype(jnp.bfloat16), "gx", scatter_dimension=0, tiled=True
        ).astype(jnp.float32),
    )
    smalls = lax.psum(
        (
            grad_gain_one,
            grad_shift_one,
            grad_qv_bias,
            grad_proj_bias,
            grad_scale_attn,
            grad_gain_two,
            grad_shift_two,
            grad_fc1_bias,
            grad_fc2_bias,
            grad_scale_mlp,
        ),
        "gx",
    )
    return (
        output,
        grad_input,
        smalls[0],
        smalls[1],
        grad_qkv,
        smalls[2],
        grad_proj,
        smalls[3],
        smalls[4],
        smalls[5],
        smalls[6],
        grad_fc1,
        smalls[7],
        grad_fc2,
        smalls[8],
        smalls[9],
    )


def solution(mesh):
    return jax.shard_map(
        on_device,
        mesh=mesh,
        in_specs=(
            P("gx", "gy"),
            P("gx", "gy"),
            P("gy"),
            P("gy"),
            P("gx", "gy"),
            P("gy"),
            P("gx", "gy"),
            P("gy"),
            P("gy"),
            P("gy"),
            P("gy"),
            P("gx", "gy"),
            P("gy"),
            P("gx", "gy"),
            P("gy"),
            P("gy"),
        ),
        out_specs=(
            P("gx", "gy"),
            P("gx", "gy"),
            P("gy"),
            P("gy"),
            P("gx", "gy"),
            P("gy"),
            P("gx", "gy"),
            P("gy"),
            P("gy"),
            P("gy"),
            P("gy"),
            P("gx", "gy"),
            P("gy"),
            P("gx", "gy"),
            P("gy"),
            P("gy"),
        ),
        check_vma=False,
    )
```

profile of v0, /device:TPU:0, one launch (start us, length us, event | category | flops | bytes accessed | tf_op | source)
XLA Modules:
  0.0 869.4 jit_solution(13419016381353141579)
XLA Ops:
  8.4 23.4 %all-reduce.3 = (f32[685]{0:T(1024)S(1)}, f32[685]{0:T(1024)S(1)}) all-reduce(f32[685]{0:T(1024)S(1)} %get-tuple-element.31, f32[685]{0:T(1024)S(1)} %get-tuple-element.30), channel_id=1, replica_groups=mesh['gx'=4,'gy'=8] {'gy'}, use_global_device_ids=true, to_apply=%region_3.0 | all-reduce | flops 1370 | bytes 10960 | tf_op jit(solution)/shard_map/psum | solution.py:37
  35.1 8.8 %all_gather.29 = bf16[1024,384]{1,0:T(8,128)(2,1)S(1)} all-gather(bf16[256,384]{1,0:T(8,128)(2,1)} %param.20), channel_id=1, replica_groups=mesh['gx'=4,'gy'=8] {'gx'}, dimensions={0}, use_global_device_ids=true | all-gather | bytes 983040 | tf_op jit(solution)/shard_map/all_gather | solution.py:94
  43.9 30.4 %all-gather.7.cloned.1.call-done = bf16[685,1024]{1,0:T(8,128)(2,1)} async-done(((bf16[685,128]{1,0:T(8,128)(2,1)}), bf16[685,1024]{1,0:T(8,128)(2,1)}) %all-gather.7.cloned.1.call-update) | async-done | bytes 1402896 | tf_op jit(solution)/shard_map/all_gather | solution.py:52
  87.4 5.8 all_gather.31
  93.2 35.4 %all-gather.9.cloned.1.call-done = bf16[685,1024]{0,1:T(8,128)(2,1)} async-done(((bf16[685,128]{0,1:T(8,128)(2,1)}), bf16[685,1024]{0,1:T(8,128)(2,1)}) %all-gather.9.cloned.1.call-update) | async-done | bytes 1402896 | tf_op jit(solution)/shard_map/all_gather | solution.py:52
  130.8 19.1 %all-reduce.2 = (f32[685]{0:T(1024)S(1)}, f32[685]{0:T(1024)S(1)}) all-reduce(f32[685]{0:T(1024)S(1)} %get-tuple-element.27, f32[685]{0:T(1024)S(1)} %get-tuple-element.26), channel_id=1, replica_groups=mesh['gx'=4,'gy'=8] {'gy'}, use_global_device_ids=true, to_apply=%region_9.10 | all-reduce | flops 1370 | bytes 10960 | tf_op jit(solution)/shard_map/psum | solution.py:37
  150.9 7.1 fusion.45
  158.1 5.3 all-gather.13.cloned.1.call-done
  163.4 45.1 %all-gather.11.cloned.1.call-done = bf16[685,1024]{1,0:T(8,128)(2,1)} async-done(((bf16[685,128]{1,0:T(8,128)(2,1)}), bf16[685,1024]{1,0:T(8,128)(2,1)}) %all-gather.11.cloned.1.call-update) | async-done | bytes 1402896 | tf_op jit(solution)/shard_map/all_gather | solution.py:52
  208.5 191.3 %reduce-scatter.9.cloned.1.call-done = f32[685,512]{1,0:T(8,128)} async-done(((f32[685,4096]{1,0:T(8,128)}), f32[685,512]{1,0:T(8,128)}) %reduce-scatter.9.cloned.1.call-update) | async-done | bytes 1402896 | tf_op jit(solution)/shard_map/reduce_scatter | solution.py:68
  399.8 5.0 fusion.60
  409.1 72.3 %reduce-scatter.11.cloned.1.call-done = f32[685,128]{1,0:T(8,128)} async-done(((f32[685,1024]{1,0:T(8,128)}), f32[685,128]{1,0:T(8,128)}) %reduce-scatter.11.cloned.1.call-update) | async-done | bytes 350736 | tf_op jit(solution)/shard_map/reduce_scatter | solution.py:68
  483.3 20.7 %all-reduce.1 = (f32[685]{0:T(1024)S(1)}, f32[685]{0:T(1024)S(1)}) all-reduce(f32[685]{0:T(1024)S(1)} %get-tuple-element.17, f32[685]{0:T(1024)S(1)} %get-tuple-element.21), channel_id=1, replica_groups=mesh['gx'=4,'gy'=8] {'gy'}, use_global_device_ids=true, to_apply=%region_15.16 | all-reduce | flops 1370 | bytes 10960 | tf_op jit(solution)/shard_map/psum | solution.py:46
  504.0 70.5 %all-gather.15.cloned.1.call-done = bf16[685,4096]{1,0:T(8,128)(2,1)} async-done(((bf16[685,512]{1,0:T(8,128)(2,1)}), bf16[685,4096]{1,0:T(8,128)(2,1)}) %all-gather.15.cloned.1.call-update) | async-done | bytes 5611536 | tf_op jit(solution)/shard_map/all_gather | solution.py:52
  574.6 5.6 fusion.26
  587.9 5.5 convolution_convert_fusion
  593.5 60.7 %reduce-scatter.13.cloned.1.call-done = f32[685,128]{1,0:T(8,128)} async-done(((f32[685,1024]{1,0:T(8,128)}), f32[685,128]{1,0:T(8,128)}) %reduce-scatter.13.cloned.1.call-update) | async-done | bytes 350736 | tf_op jit(solution)/shard_map/reduce_scatter | solution.py:68
  659.8 6.2 multiply_convert_fusion
  682.3 20.8 %reduce-scatter.19.cloned.1.call-done = bf16[256,128]{1,0:T(8,128)(2,1)} async-done(((bf16[1024,128]{1,0:T(8,128)(2,1)}), bf16[256,128]{1,0:T(8,128)(2,1)}) %reduce-scatter.19.cloned.1.call-update) | async-done | bytes 65552 | tf_op jit(solution)/shard_map/reduce_scatter | solution.py:210
  704.6 25.7 %reduce-scatter.23.cloned.1.call-done = bf16[1024,128]{1,0:T(8,128)(2,1)} async-done(((bf16[4096,128]{1,0:T(8,128)(2,1)}), bf16[1024,128]{1,0:T(8,128)(2,1)}) %reduce-scatter.23.cloned.1.call-update) | async-done | bytes 262160 | tf_op jit(solution)/shard_map/reduce_scatter | solution.py:216
  732.3 23.8 %reduce-scatter.17.cloned.1.call-done = bf16[256,384]{1,0:T(8,128)(2,1)} async-done(((bf16[1024,384]{1,0:T(8,128)(2,1)}), bf16[256,384]{1,0:T(8,128)(2,1)}) %reduce-scatter.17.cloned.1.call-update) | async-done | bytes 196624 | tf_op jit(solution)/shard_map/reduce_scatter | solution.py:207
  757.8 75.2 %reduce-scatter.15.cloned.1.call-done = f32[685,128]{1,0:T(8,128)} async-done(((f32[685,1024]{1,0:T(8,128)}), f32[685,128]{1,0:T(8,128)}) %reduce-scatter.15.cloned.1.call-update) | async-done | bytes 350736 | tf_op jit(solution)/shard_map/reduce_scatter | solution.py:68
  834.5 19.8 %all-reduce = (f32[685]{0:T(1024)S(1)}, f32[685]{0:T(1024)S(1)}) all-reduce(f32[685]{0:T(1024)S(1)} %get-tuple-element.19, f32[685]{0:T(1024)S(1)} %get-tuple-element.20), channel_id=1, replica_groups=mesh['gx'=4,'gy'=8] {'gy'}, use_global_device_ids=true, to_apply=%region_22.23 | all-reduce | flops 1370 | bytes 10960 | tf_op jit(solution)/shard_map/psum | solution.py:46
  854.4 6.3 all-reduce.4
  (175 shorter events, 64.8 us)
Async XLA Ops:
  7.2 67.2 %all-gather.7.cloned.1.call-start = ((), (), s32[]{:S(2)}) async-start(), calls=%async_computation.8 | async-start | bytes 1585152 | tf_op jit(solution)/shard_map/all_gather | solution.py:52
  34.3 94.2 %all-gather.9.cloned.1.call-start = ((), (), s32[]{:S(2)}) async-start(), calls=%async_computation.9 | async-start | bytes 1769472 | tf_op jit(solution)/shard_map/all_gather | solution.py:52
  76.7 1.8 collective-permute-start
  86.0 64.9 %all-gather.17.cloned.1.call-start = ((), (), s32[]{:S(2)}) async-start(), calls=%async_computation.13 | async-start | bytes 1310720 | tf_op jit(solution)/shard_map/all_gather | solution.py:97
  86.7 76.6 %all-gather.13.cloned.1.call-start = ((), (), s32[]{:S(2)}) async-start(), calls=%async_computation.11 | async-start | bytes 1310720 | tf_op jit(solution)/shard_map/all_gather | solution.py:96
  87.3 121.2 %all-gather.11.cloned.1.call-start = ((), (), s32[]{:S(2)}) async-start(), calls=%async_computation.10 | async-start | bytes 1585152 | tf_op jit(solution)/shard_map/all_gather | solution.py:52
  150.8 249.0 %reduce-scatter.9.cloned.1.call-start = ((), (), s32[]{:S(2)}) async-start(), calls=%async_computation.14 | async-start | bytes 12681216 | tf_op jit(solution)/shard_map/reduce_scatter | solution.py:68
  158.0 241.8 %copy-start.42 = (f32[512]{0:T(512)S(1)}, f32[512]{0:T(512)}, u32[]{:S(2)}) copy-start(f32[512]{0:T(512)} %param.28) | copy-start | bytes 6148
  158.1 323.3 %reduce-scatter.11.cloned.1.call-start = ((), (), s32[]{:S(2)}) async-start(), calls=%async_computation.15 | async-start | bytes 3170304 | tf_op jit(solution)/shard_map/reduce_scatter | solution.py:68
  163.4 242.4 %copy-start.15 = (bf16[1024,512]{1,0:T(8,128)(2,1)S(1)}, bf16[1024,512]{1,0:T(8,128)(2,1)}, u32[]{:S(2)}) copy-start(bf16[1024,512]{1,0:T(8,128)(2,1)} %all-gather.13.cloned.1.call-done) | copy-start | bytes 3145732
  408.3 166.3 %all-gather.15.cloned.1.call-start = ((), (), s32[]{:S(2)}) async-start(), calls=%async_computation.12 | async-start | bytes 6340608 | tf_op jit(solution)/shard_map/all_gather | solution.py:52
  409.0 245.2 %reduce-scatter.13.cloned.1.call-start = ((), (), s32[]{:S(2)}) async-start(), calls=%async_computation.16 | async-start | bytes 3170304 | tf_op jit(solution)/shard_map/reduce_scatter | solution.py:68
  582.4 98.2 %reduce-scatter.21.cloned.1.call-start = ((), (), s32[]{:S(2)}) async-start(), calls=%async_computation.20 | async-start | bytes 1310720 | tf_op jit(solution)/shard_map/reduce_scatter | solution.py:213
  585.9 117.2 %reduce-scatter.19.cloned.1.call-start = ((), (), s32[]{:S(2)}) async-start(), calls=%async_computation.19 | async-start | bytes 327680 | tf_op jit(solution)/shard_map/reduce_scatter | solution.py:210
  587.3 143.0 %reduce-scatter.23.cloned.1.call-start = ((), (), s32[]{:S(2)}) async-start(), calls=%async_computation.21 | async-start | bytes 1310720 | tf_op jit(solution)/shard_map/reduce_scatter | solution.py:216
  593.5 162.6 %reduce-scatter.17.cloned.1.call-start = ((), (), s32[]{:S(2)}) async-start(), calls=%async_computation.18 | async-start | bytes 983040 | tf_op jit(solution)/shard_map/reduce_scatter | solution.py:207
  669.9 2.3 collective-permute-start.1
  675.6 157.4 %reduce-scatter.15.cloned.1.call-start = ((), (), s32[]{:S(2)}) async-start(), calls=%async_computation.17 | async-start | bytes 3170304 | tf_op jit(solution)/shard_map/reduce_scatter | solution.py:68
  678.2 176.1 %copy-start.31 = (f32[128]{0:T(128)S(1)}, f32[128]{0:T(128)}, u32[]{:S(2)}) copy-start(f32[128]{0:T(128)} %get-tuple-element.16) | copy-start | bytes 1540
  678.2 176.1 %copy-start.32 = (f32[128]{0:T(128)S(1)}, f32[128]{0:T(128)}, u32[]{:S(2)}) copy-start(f32[128]{0:T(128)} %get-tuple-element.22) | copy-start | bytes 1540
  678.2 176.1 %copy-start.33 = (f32[512]{0:T(512)S(1)}, f32[512]{0:T(512)}, u32[]{:S(2)}) copy-start(f32[512]{0:T(512)} %get-tuple-element.50) | copy-start | bytes 6148
  678.2 176.1 %copy-start.36 = (f32[128]{0:T(128)S(1)}, f32[128]{0:T(128)}, u32[]{:S(2)}) copy-start(f32[128]{0:T(128)} %get-tuple-element.28) | copy-start | bytes 1540
  678.2 176.1 %copy-start.37 = (f32[128]{0:T(128)S(1)}, f32[128]{0:T(128)}, u32[]{:S(2)}) copy-start(f32[128]{0:T(128)} %get-tuple-element.29) | copy-start | bytes 1540
  678.2 182.5 %copy-start.9 = (f32[685,128]{1,0:T(8,128)S(1)}, f32[685,128]{1,0:T(8,128)}, u32[]{:S(2)}) copy-start(f32[685,128]{1,0:T(8,128)} %copy-done.8) | copy-start | bytes 1052164
  (38 other events, 1841.7 us)
Sparse Core Ops, SparseCore 0:
  34.4 39.8 all-gather.6
  86.1 42.3 all-gather.8
  130.1 15.0 all-gather.16
  146.6 16.6 all-gather.12
  165.8 42.6 all-gather.10
  212.0 187.7 reduce-scatter.8
  408.4 72.9 reduce-scatter.10
  483.4 91.1 all-gather.14
  582.5 71.7 reduce-scatter.12
  656.6 23.8 reduce-scatter.20
  683.0 20.0 reduce-scatter.18
  705.5 24.7 reduce-scatter.22
  732.8 23.2 reduce-scatter.16
  759.5 73.5 reduce-scatter.14
where the time goes:
time: 870 us; the launch traced here: 869 us
  waiting for transfers between devices  663 us (76%)
  blocking collectives  104 us (12%)
  matrix products  56.9 us (7%)
  other arithmetic  21.6 us (2%)
  between operations  14.6 us (2%)
  local copies, waits for them, and re-layouts  9.18 us (1%)
    reduce_scatter x4, waiting for transfers between devices, back_project(): return lax.psum_scatter(term, 'gy', scatter_dimension=1, tiled=True)  400 us
    all_gather x4, waiting for transfers between devices, project(): lax.all_gather(inputs, 'gy', axis=1, tiled=True)  181 us
    psum x2, blocking collectives, norm_forward(): lax.psum((jnp.sum(rows, axis=1), jnp.sum(rows * rows, axis=1)), 'gy')  42.5 us
    psum x2, blocking collectives, norm_backward(): lax.psum((jnp.sum(scaled, axis=1), jnp.sum(scaled * normed, axis=1)), 'gy')  40.4 us
    reduce_scatter x1, waiting for transfers between devices, on_device(): lax.psum_scatter(grad_fc2.astype(jnp.bfloat16), 'gx', scatter_dimension=0...  25.7 us
    reduce_scatter x1, waiting for transfers between devices, on_device(): lax.psum_scatter(grad_qkv.astype(jnp.bfloat16), 'gx', scatter_dimension=0...  23.8 us
    reduce_scatter x1, waiting for transfers between devices, on_device(): lax.psum_scatter(grad_proj.astype(jnp.bfloat16), 'gx', scatter_dimension=...  20.8 us
  transfers between devices with their start and end apart: 16, of which 14 were waited for; matrix products, arithmetic and copies ran while one was open for 6% of the time, Pallas kernels for 0%

commit v1 on v0

--- a/solution.py
+++ b/solution.py
@@ -9,6 +9,28 @@
 EPS = 1e-06
 ROOT_HALF = 0.7071067811865476
 INV_ROOT_TAU = 0.3989422804014327
+
+
+def in_order(parts, dim):
+    lengths = list(parts.shape[1:])
+    lengths[dim] *= parts.shape[0]
+    return jnp.moveaxis(parts, 0, dim).reshape(lengths)
+
+
+def ring_gather(array, axis, dim):
+    size = lax.axis_size(axis)
+    pairs = [(i, (i + 1) % size) for i in range(size)]
+    back = [(b, a) for a, b in pairs]
+    lower, upper = ([], [])
+    for step in range(size - 1):
+        if step % 2 == 0:
+            lower.append(lax.ppermute(lower[-1] if lower else array, axis, pairs))
+        else:
+            upper.append(lax.ppermute(upper[-1] if upper else array, axis, back))
+    tiles = jnp.stack([*lower[::-1], array, *upper])
+    shift = lax.axis_index(axis) - len(lower)
+    tiles = tiles[(jnp.arange(size) - shift) % size]
+    return in_order(tiles, dim)
 
 
 def from_partner(block, axis, bit):
@@ -48,9 +70,7 @@
 
 
 def project(inputs, weight):
-    result = jnp.dot(
-        lax.all_gather(inputs, "gy", axis=1, tiled=True), weight, preferred_element_type=jnp.float32
-    )
+    result = jnp.dot(ring_gather(inputs, "gy", 1), weight, preferred_element_type=jnp.float32)
     return (result, inputs)
 
 

time: 870 us -> 966 us (1.11)
  starting transfers between devices: 0.71 us -> 73.9 us
  waiting for transfers between devices: 663 us -> 619 us
  local copies, waits for them, and re-layouts: 9.18 us -> 52.8 us
  blocking collectives: 104 us -> 118 us
    reduce_scatter x4, waiting for transfers between devices: 400 us -> 147 us  [back_project(): return lax.psum_scatter(term, 'gy', scatter_dimension=1, tiled=True)]
    ppermute x0 -> x28, waiting for transfers between devices: none -> 212 us  [the longest x16 153 us: ring_gather(): lower.append(lax.ppermute(lower[-1] if lower else array, axis, pairs))]
    ppermute x0 -> x28, starting transfers between devices: none -> 73 us  [the longest x12 66.6 us: ring_gather(): upper.append(lax.ppermute(upper[-1] if upper else array, axis, back))]
    all_gather x4, waiting for transfers between devices: 181 us -> 145 us  [weight_grad(): lax.all_gather(saved, 'gy', axis=1, tiled=True)]
    unnamed x92 -> x128, local copies, waits for them, and re-layouts: 5.52 us -> 26.3 us
    all_gather x1, waiting for transfers between devices: 0.02 us -> 20.3 us  [on_device(): lax.all_gather(fc2_weight, 'gx', axis=0, tiled=True)]
    reduce_scatter x1, waiting for transfers between devices: 2.24 us -> 19.3 us  [on_device(): lax.psum_scatter(grad_fc1.astype(jnp.bfloat16), 'gx', scatter_dimension=0...]
    psum x2, blocking collectives: 42.5 us -> 55.2 us  [norm_forward(): lax.psum((jnp.sum(rows, axis=1), jnp.sum(rows * rows, axis=1)), 'gy')]
  transfers between devices with their start and end apart: 16 -> 44, of which waited for: 14 -> 29; matrix products, arithmetic and copies ran while one was open for 6% -> 12% of each run, Pallas kernels for 0% -> 0%
where the time goes in v1:
time: 966 us; the launch traced here: 957 us
  waiting for transfers between devices  619 us (64%)
  blocking collectives  118 us (12%)
  starting transfers between devices  73.9 us (8%)
  matrix products  57.4 us (6%)
  local copies, waits for them, and re-layouts  52.8 us (5%)
  other arithmetic  20.4 us (2%)
  between operations  15.4 us (2%)
    ppermute x16, waiting for transfers between devices, ring_gather(): lower.append(lax.ppermute(lower[-1] if lower else array, axis, pairs))  153 us
    reduce_scatter x4, waiting for transfers between devices, back_project(): return lax.psum_scatter(term, 'gy', scatter_dimension=1, tiled=True)  147 us
    all_gather x4, waiting for transfers between devices, weight_grad(): lax.all_gather(saved, 'gy', axis=1, tiled=True)  145 us
    ppermute x12, starting transfers between devices, ring_gather(): upper.append(lax.ppermute(upper[-1] if upper else array, axis, back))  66.6 us
    ppermute x12, waiting for transfers between devices, ring_gather(): upper.append(lax.ppermute(upper[-1] if upper else array, axis, back))  58.1 us
    psum x2, blocking collectives, norm_forward(): lax.psum((jnp.sum(rows, axis=1), jnp.sum(rows * rows, axis=1)), 'gy')  55.2 us
    psum x2, blocking collectives, norm_backward(): lax.psum((jnp.sum(scaled, axis=1), jnp.sum(scaled * normed, axis=1)), 'gy')  43.1 us
    unnamed x128, local copies, waits for them, and re-layouts  26.3 us
  transfers between devices with their start and end apart: 44, of which 29 were waited for; matrix products, arithmetic and copies ran while one was open for 12% of the time, Pallas kernels for 0%

profile of v1, /device:TPU:0, one launch (start us, length us, event | category | flops | bytes accessed | tf_op | source)
XLA Modules:
  0.0 956.8 jit_solution(11849151248260421216)
XLA Ops:
  8.7 20.3 %all-gather.9.cloned.1.call-done = bf16[4096,128]{1,0:T(8,128)(2,1)} async-done(((bf16[1024,128]{1,0:T(8,128)(2,1)}), bf16[4096,128]{1,0:T(8,128)(2,1)}) %all-gather.9.cloned.1.call-update) | async-done | bytes 1048592 | tf_op jit(solution)/shard_map/all_gather | solution.py:117
  37.4 21.7 %all-reduce.3 = (f32[685]{0:T(1024)S(1)}, f32[685]{0:T(1024)S(1)}) all-reduce(f32[685]{0:T(1024)S(1)} %get-tuple-element.31, f32[685]{0:T(1024)S(1)} %get-tuple-element.30), channel_id=1, replica_groups=mesh['gx'=4,'gy'=8] {'gy'}, use_global_device_ids=true, to_apply=%region_3.0 | all-reduce | flops 1370 | bytes 10960 | tf_op jit(solution)/shard_map/psum | solution.py:59
  125.8 13.4 %collective-permute-done.8 = bf16[685,128]{0,1:T(8,128)(2,1)S(1)} collective-permute-done((bf16[685,128]{0,1:T(8,128)(2,1)S(1)}, bf16[685,128]{0,1:T(8,128)(2,1)S(1)}, u32[]{:S(2)}, u32[]{:S(2)}) %collective-permute-start.8) | collective-permute-done | bytes 175392 | tf_op jit(solution)/shard_map/ppermute | solution.py:27
  143.9 9.5 collective-permute-done.9
  159.2 9.7 %collective-permute-done.10 = bf16[685,128]{0,1:T(8,128)(2,1)S(1)} collective-permute-done((bf16[685,128]{0,1:T(8,128)(2,1)S(1)}, bf16[685,128]{0,1:T(8,128)(2,1)S(1)}, u32[]{:S(2)}, u32[]{:S(2)}) %collective-permute-start.10) | collective-permute-done | bytes 175392 | tf_op jit(solution)/shard_map/ppermute | solution.py:27
  174.7 11.5 %collective-permute-start.14 = (bf16[685,128]{0,1:T(8,128)(2,1)S(1)}, bf16[685,128]{0,1:T(8,128)(2,1)S(1)}, u32[]{:S(2)}, u32[]{:S(2)}) collective-permute-start(bf16[685,128]{0,1:T(8,128)(2,1)S(1)} %collective-permute-done.13), channel_id=1, source_target_pairs={{1,0},{2,1},{3,2},{4,3},{5,4},{6,5},{7,6},{0,7},{9,8},{10,9},{11,1... | collective-permute-start | bytes 526088 | tf_op jit(solution)/shard_map/ppermute | solution.py:29
  197.1 33.5 %all-reduce.2 = (f32[685]{0:T(1024)S(1)}, f32[685]{0:T(1024)S(1)}) all-reduce(f32[685]{0:T(1024)S(1)} %get-tuple-element.27, f32[685]{0:T(1024)S(1)} %get-tuple-element.26), channel_id=1, replica_groups=mesh['gx'=4,'gy'=8] {'gy'}, use_global_device_ids=true, to_apply=%region_9.10 | all-reduce | flops 1370 | bytes 10960 | tf_op jit(solution)/shard_map/psum | solution.py:59
  231.1 13.5 %collective-permute-done.15 = bf16[685,128]{1,0:T(8,128)(2,1)S(1)} collective-permute-done((bf16[685,128]{1,0:T(8,128)(2,1)S(1)}, bf16[685,128]{1,0:T(8,128)(2,1)S(1)}, u32[]{:S(2)}, u32[]{:S(2)}) %collective-permute-start.15) | collective-permute-done | bytes 175392 | tf_op jit(solution)/shard_map/ppermute | solution.py:27
  249.3 9.3 collective-permute-done.16
  304.4 29.4 %collective-permute-done.22 = bf16[685,512]{1,0:T(8,128)(2,1)S(1)} collective-permute-done((bf16[685,512]{1,0:T(8,128)(2,1)S(1)}, bf16[685,512]{1,0:T(8,128)(2,1)S(1)}, u32[]{:S(2)}, u32[]{:S(2)}) %collective-permute-start.22) | collective-permute-done | bytes 701472 | tf_op jit(solution)/shard_map/ppermute | solution.py:27
  338.6 25.5 %collective-permute-done.23 = bf16[685,512]{1,0:T(8,128)(2,1)S(1)} collective-permute-done((bf16[685,512]{1,0:T(8,128)(2,1)S(1)}, bf16[685,512]{1,0:T(8,128)(2,1)S(1)}, u32[]{:S(2)}, u32[]{:S(2)}) %collective-permute-start.23) | collective-permute-done | bytes 701472 | tf_op jit(solution)/shard_map/ppermute | solution.py:27
  366.5 22.1 %collective-permute-done.26 = bf16[685,512]{1,0:T(8,128)(2,1)S(1)} collective-permute-done((bf16[685,512]{1,0:T(8,128)(2,1)S(1)}, bf16[685,512]{1,0:T(8,128)(2,1)S(1)}, u32[]{:S(2)}, u32[]{:S(2)}) %collective-permute-start.26) | collective-permute-done | bytes 701472 | tf_op jit(solution)/shard_map/ppermute | solution.py:29
  397.2 25.1 %collective-permute-done.27 = bf16[685,512]{1,0:T(8,128)(2,1)S(1)} collective-permute-done((bf16[685,512]{1,0:T(8,128)(2,1)S(1)}, bf16[685,512]{1,0:T(8,128)(2,1)S(1)}, u32[]{:S(2)}, u32[]{:S(2)}) %collective-permute-start.27) | collective-permute-done | bytes 701472 | tf_op jit(solution)/shard_map/ppermute | solution.py:29
  462.2 23.3 %all-reduce.1 = (f32[685]{0:T(1024)S(1)}, f32[685]{0:T(1024)S(1)}) all-reduce(f32[685]{0:T(1024)S(1)} %get-tuple-element.17, f32[685]{0:T(1024)S(1)} %get-tuple-element.21), channel_id=1, replica_groups=mesh['gx'=4,'gy'=8] {'gy'}, use_global_device_ids=true, to_apply=%region_15.16 | all-reduce | flops 1370 | bytes 10960 | tf_op jit(solution)/shard_map/psum | solution.py:68
  497.9 31.5 %all-gather.13.cloned.1.call-done = bf16[685,1024]{0,1:T(8,128)(2,1)} async-done(((bf16[685,128]{0,1:T(8,128)(2,1)}), bf16[685,1024]{0,1:T(8,128)(2,1)}) %all-gather.13.cloned.1.call-update) | async-done | bytes 1402896 | tf_op jit(solution)/shard_map/all_gather | solution.py:80
  532.7 88.6 %all-gather.17.cloned.1.call-done = bf16[685,4096]{1,0:T(8,128)(2,1)} async-done(((bf16[685,512]{1,0:T(8,128)(2,1)}), bf16[685,4096]{1,0:T(8,128)(2,1)}) %all-gather.17.cloned.1.call-update) | async-done | bytes 5611536 | tf_op jit(solution)/shard_map/all_gather | solution.py:80
  626.9 70.5 %reduce-scatter.13.cloned.1.call-done = f32[685,128]{1,0:T(8,128)} async-done(((f32[685,1024]{1,0:T(8,128)}), f32[685,128]{1,0:T(8,128)}) %reduce-scatter.13.cloned.1.call-update) | async-done | bytes 350736 | tf_op jit(solution)/shard_map/reduce_scatter | solution.py:88
  716.4 24.8 %all-gather.11.cloned.1.call-done = bf16[685,1024]{1,0:T(8,128)(2,1)} async-done(((bf16[685,128]{1,0:T(8,128)(2,1)}), bf16[685,1024]{1,0:T(8,128)(2,1)}) %all-gather.11.cloned.1.call-update) | async-done | bytes 1402896 | tf_op jit(solution)/shard_map/all_gather | solution.py:80
  747.3 19.3 %reduce-scatter.21.cloned.1.call-done = bf16[256,512]{1,0:T(8,128)(2,1)} async-done(((bf16[1024,512]{1,0:T(8,128)(2,1)}), bf16[256,512]{1,0:T(8,128)(2,1)}) %reduce-scatter.21.cloned.1.call-update) | async-done | bytes 262160 | tf_op jit(solution)/shard_map/reduce_scatter | solution.py:233
  768.4 20.8 %reduce-scatter.19.cloned.1.call-done = bf16[256,128]{1,0:T(8,128)(2,1)} async-done(((bf16[1024,128]{1,0:T(8,128)(2,1)}), bf16[256,128]{1,0:T(8,128)(2,1)}) %reduce-scatter.19.cloned.1.call-update) | async-done | bytes 65552 | tf_op jit(solution)/shard_map/reduce_scatter | solution.py:230
  790.8 25.5 %reduce-scatter.23.cloned.1.call-done = bf16[1024,128]{1,0:T(8,128)(2,1)} async-done(((bf16[4096,128]{1,0:T(8,128)(2,1)}), bf16[1024,128]{1,0:T(8,128)(2,1)}) %reduce-scatter.23.cloned.1.call-update) | async-done | bytes 262160 | tf_op jit(solution)/shard_map/reduce_scatter | solution.py:236
  818.1 24.0 %reduce-scatter.17.cloned.1.call-done = bf16[256,384]{1,0:T(8,128)(2,1)} async-done(((bf16[1024,384]{1,0:T(8,128)(2,1)}), bf16[256,384]{1,0:T(8,128)(2,1)}) %reduce-scatter.17.cloned.1.call-update) | async-done | bytes 196624 | tf_op jit(solution)/shard_map/reduce_scatter | solution.py:227
  843.8 76.2 %reduce-scatter.15.cloned.1.call-done = f32[685,128]{1,0:T(8,128)} async-done(((f32[685,1024]{1,0:T(8,128)}), f32[685,128]{1,0:T(8,128)}) %reduce-scatter.15.cloned.1.call-update) | async-done | bytes 350736 | tf_op jit(solution)/shard_map/reduce_scatter | solution.py:88
  921.5 19.8 %all-reduce = (f32[685]{0:T(1024)S(1)}, f32[685]{0:T(1024)S(1)}) all-reduce(f32[685]{0:T(1024)S(1)} %get-tuple-element.19, f32[685]{0:T(1024)S(1)} %get-tuple-element.20), channel_id=1, replica_groups=mesh['gx'=4,'gy'=8] {'gy'}, use_global_device_ids=true, to_apply=%region_22.23 | all-reduce | flops 1370 | bytes 10960 | tf_op jit(solution)/shard_map/psum | solution.py:68
  (284 shorter events, 272.7 us)
Async XLA Ops:
  7.2 21.8 %all-gather.9.cloned.1.call-start = ((), (), s32[]{:S(2)}) async-start(), calls=%async_computation.9 | async-start | bytes 1310720 | tf_op jit(solution)/shard_map/all_gather | solution.py:117
  7.9 285.0 %all-gather.7.cloned.1.call-start = ((), (), s32[]{:S(2)}) async-start(), calls=%async_computation.8 | async-start | bytes 1310720 | tf_op jit(solution)/shard_map/all_gather | solution.py:116
  8.7 284.3 %reduce-scatter.9.cloned.1.call-start = ((), (), s32[]{:S(2)}) async-start(), calls=%async_computation.10 | async-start | bytes 12681216 | tf_op jit(solution)/shard_map/reduce_scatter | solution.py:88
  36.3 424.0 %reduce-scatter.11.cloned.1.call-start = ((), (), s32[]{:S(2)}) async-start(), calls=%async_computation.11 | async-start | bytes 3170304 | tf_op jit(solution)/shard_map/reduce_scatter | solution.py:88
  59.5 25.2 %collective-permute-start.4 = (bf16[685,128]{1,0:T(8,128)(2,1)S(1)}, bf16[685,128]{1,0:T(8,128)(2,1)S(1)}, u32[]{:S(2)}, u32[]{:S(2)}) collective-permute-start(bf16[685,128]{1,0:T(8,128)(2,1)S(1)} %fusion.35), channel_id=1, source_target_pairs={{1,0},{2,1},{3,2},{4,3},{5,4},{6,5},{7,6},{0,7},{9,8},{10,9},{11,1... | collective-permute-start | bytes 526088 | tf_op jit(solution)/shard_map/ppermute | solution.py:29
  153.4 21.3 %collective-permute-start.13 = (bf16[685,128]{0,1:T(8,128)(2,1)S(1)}, bf16[685,128]{0,1:T(8,128)(2,1)S(1)}, u32[]{:S(2)}, u32[]{:S(2)}) collective-permute-start(bf16[685,128]{0,1:T(8,128)(2,1)S(1)} %collective-permute-done.12), channel_id=1, source_target_pairs={{1,0},{2,1},{3,2},{4,3},{5,4},{6,5},{7,6},{0,7},{9,8},{10,9},{11,1... | collective-permute-start | bytes 526088 | tf_op jit(solution)/shard_map/ppermute | solution.py:29
  174.7 18.8 %collective-permute-start.14 = (bf16[685,128]{0,1:T(8,128)(2,1)S(1)}, bf16[685,128]{0,1:T(8,128)(2,1)S(1)}, u32[]{:S(2)}, u32[]{:S(2)}) collective-permute-start(bf16[685,128]{0,1:T(8,128)(2,1)S(1)} %collective-permute-done.13), channel_id=1, source_target_pairs={{1,0},{2,1},{3,2},{4,3},{5,4},{6,5},{7,6},{0,7},{9,8},{10,9},{11,1... | collective-permute-start | bytes 526088 | tf_op jit(solution)/shard_map/ppermute | solution.py:29
  300.5 194.0 %all-gather.15.cloned.1.call-start = ((), (), s32[]{:S(2)}) async-start(), calls=%async_computation.18 | async-start | bytes 1585152 | tf_op jit(solution)/shard_map/all_gather | solution.py:80
  301.1 228.3 %all-gather.13.cloned.1.call-start = ((), (), s32[]{:S(2)}) async-start(), calls=%async_computation.16 | async-start | bytes 1769472 | tf_op jit(solution)/shard_map/all_gather | solution.py:80
  301.6 319.7 %all-gather.17.cloned.1.call-start = ((), (), s32[]{:S(2)}) async-start(), calls=%async_computation.20 | async-start | bytes 6340608 | tf_op jit(solution)/shard_map/all_gather | solution.py:80
  302.4 395.0 %reduce-scatter.13.cloned.1.call-start = ((), (), s32[]{:S(2)}) async-start(), calls=%async_computation.12 | async-start | bytes 3170304 | tf_op jit(solution)/shard_map/reduce_scatter | solution.py:88
  302.4 31.4 %collective-permute-start.22 = (bf16[685,512]{1,0:T(8,128)(2,1)S(1)}, bf16[685,512]{1,0:T(8,128)(2,1)S(1)}, u32[]{:S(2)}, u32[]{:S(2)}) collective-permute-start(bf16[685,512]{1,0:T(8,128)(2,1)S(1)} %copy-done.11), channel_id=1, source_target_pairs={{0,1},{1,2},{2,3},{3,4},{4,5},{5,6},{6,7},{7,0},{8,9},{9,10},{10,1... | collective-permute-start | bytes 2104328 | tf_op jit(solution)/shard_map/ppermute | solution.py:27
  333.8 30.2 %collective-permute-start.23 = (bf16[685,512]{1,0:T(8,128)(2,1)S(1)}, bf16[685,512]{1,0:T(8,128)(2,1)S(1)}, u32[]{:S(2)}, u32[]{:S(2)}) collective-permute-start(bf16[685,512]{1,0:T(8,128)(2,1)S(1)} %collective-permute-done.22), channel_id=1, source_target_pairs={{0,1},{1,2},{2,3},{3,4},{4,5},{5,6},{6,7},{7,0},{8,9},{9,10},{10,1... | collective-permute-start | bytes 2104328 | tf_op jit(solution)/shard_map/ppermute | solution.py:27
  333.8 54.8 %collective-permute-start.26 = (bf16[685,512]{1,0:T(8,128)(2,1)S(1)}, bf16[685,512]{1,0:T(8,128)(2,1)S(1)}, u32[]{:S(2)}, u32[]{:S(2)}) collective-permute-start(bf16[685,512]{1,0:T(8,128)(2,1)S(1)} %copy-done.11), channel_id=1, source_target_pairs={{1,0},{2,1},{3,2},{4,3},{5,4},{6,5},{7,6},{0,7},{9,8},{10,9},{11,1... | collective-permute-start | bytes 2104328 | tf_op jit(solution)/shard_map/ppermute | solution.py:29
  364.0 33.1 %collective-permute-start.24 = (bf16[685,512]{1,0:T(8,128)(2,1)S(1)}, bf16[685,512]{1,0:T(8,128)(2,1)S(1)}, u32[]{:S(2)}, u32[]{:S(2)}) collective-permute-start(bf16[685,512]{1,0:T(8,128)(2,1)S(1)} %collective-permute-done.23), channel_id=1, source_target_pairs={{0,1},{1,2},{2,3},{3,4},{4,5},{5,6},{6,7},{7,0},{8,9},{9,10},{10,1... | collective-permute-start | bytes 2104328 | tf_op jit(solution)/shard_map/ppermute | solution.py:27
  388.6 33.7 %collective-permute-start.27 = (bf16[685,512]{1,0:T(8,128)(2,1)S(1)}, bf16[685,512]{1,0:T(8,128)(2,1)S(1)}, u32[]{:S(2)}, u32[]{:S(2)}) collective-permute-start(bf16[685,512]{1,0:T(8,128)(2,1)S(1)} %collective-permute-done.26), channel_id=1, source_target_pairs={{1,0},{2,1},{3,2},{4,3},{5,4},{6,5},{7,6},{0,7},{9,8},{10,9},{11,1... | collective-permute-start | bytes 2104328 | tf_op jit(solution)/shard_map/ppermute | solution.py:29
  397.2 29.0 %collective-permute-start.25 = (bf16[685,512]{1,0:T(8,128)(2,1)S(1)}, bf16[685,512]{1,0:T(8,128)(2,1)S(1)}, u32[]{:S(2)}, u32[]{:S(2)}) collective-permute-start(bf16[685,512]{1,0:T(8,128)(2,1)S(1)} %collective-permute-done.24), channel_id=1, source_target_pairs={{0,1},{1,2},{2,3},{3,4},{4,5},{5,6},{6,7},{7,0},{8,9},{9,10},{10,1... | collective-permute-start | bytes 2104328 | tf_op jit(solution)/shard_map/ppermute | solution.py:27
  422.3 18.5 %collective-permute-start.28 = (bf16[685,512]{1,0:T(8,128)(2,1)S(1)}, bf16[685,512]{1,0:T(8,128)(2,1)S(1)}, u32[]{:S(2)}, u32[]{:S(2)}) collective-permute-start(bf16[685,512]{1,0:T(8,128)(2,1)S(1)} %collective-permute-done.27), channel_id=1, source_target_pairs={{1,0},{2,1},{3,2},{4,3},{5,4},{6,5},{7,6},{0,7},{9,8},{10,9},{11,1... | collective-permute-start | bytes 2104328 | tf_op jit(solution)/shard_map/ppermute | solution.py:29
  493.4 247.7 %all-gather.11.cloned.1.call-start = ((), (), s32[]{:S(2)}) async-start(), calls=%async_computation.14 | async-start | bytes 1585152 | tf_op jit(solution)/shard_map/all_gather | solution.py:80
  494.2 272.4 %reduce-scatter.21.cloned.1.call-start = ((), (), s32[]{:S(2)}) async-start(), calls=%async_computation.19 | async-start | bytes 1310720 | tf_op jit(solution)/shard_map/reduce_scatter | solution.py:233
  497.8 291.3 %reduce-scatter.19.cloned.1.call-start = ((), (), s32[]{:S(2)}) async-start(), calls=%async_computation.17 | async-start | bytes 327680 | tf_op jit(solution)/shard_map/reduce_scatter | solution.py:230
  532.1 284.2 %reduce-scatter.23.cloned.1.call-start = ((), (), s32[]{:S(2)}) async-start(), calls=%async_computation.21 | async-start | bytes 1310720 | tf_op jit(solution)/shard_map/reduce_scatter | solution.py:236
  626.9 215.2 %reduce-scatter.17.cloned.1.call-start = ((), (), s32[]{:S(2)}) async-start(), calls=%async_computation.15 | async-start | bytes 983040 | tf_op jit(solution)/shard_map/reduce_scatter | solution.py:227
  744.5 175.5 %reduce-scatter.15.cloned.1.call-start = ((), (), s32[]{:S(2)}) async-start(), calls=%async_computation.13 | async-start | bytes 3170304 | tf_op jit(solution)/shard_map/reduce_scatter | solution.py:88
  (69 other events, 3313.3 us)
Sparse Core Ops, SparseCore 0:
  9.5 19.4 all-gather.8
  30.6 16.6 all-gather.6
  51.0 240.5 reduce-scatter.8
  300.6 131.7 reduce-scatter.10
  434.8 49.9 all-gather.14
  486.9 42.3 all-gather.12
  531.4 89.8 all-gather.16
  624.8 72.4 reduce-scatter.12
  699.4 41.6 all-gather.10
  743.5 22.9 reduce-scatter.20
  769.0 20.0 reduce-scatter.18
  791.5 24.7 reduce-scatter.22
  818.9 23.1 reduce-scatter.16
  845.5 74.5 reduce-scatter.14
